TPU v7x, 32 devices: a whole 2x2x4 slice. The times are simulated.
32 devices in a mesh: dp: 4 (over z), expert: 8 (over y, x, core).
Axes of the slice: x: 2, y: 2, z: 4, core: 2. Of those that a mesh axis runs over, the one named last changes fastest.
Arguments:
- tokens: bfloat16 [4096, 4096], P(('dp', 'expert')), may hold values from -6 to 6
- chosen: int32 [32, 128], replicated, may hold values from 0 to 4095, as said below
- gate_levels: int32 [32, 128], replicated, may hold values from 32 to 255
- expert_gate: bfloat16 [32, 4096, 768], P(('dp', 'expert')), may hold values from -0.09375 to 0.09375
- expert_up: bfloat16 [32, 4096, 768], P(('dp', 'expert')), may hold values from -0.09375 to 0.09375
- expert_down: bfloat16 [32, 768, 4096], P(('dp', 'expert')), may hold values from -0.21875 to 0.21875
- shared_gate: bfloat16 [4096, 4096], P(('dp', 'expert')), may hold values from -0.09375 to 0.09375
- shared_up: bfloat16 [4096, 4096], P(('dp', 'expert')), may hold values from -0.09375 to 0.09375
- shared_down: bfloat16 [4096, 4096], P(('dp', 'expert')), may hold values from -0.09375 to 0.09375
Outputs:
- block_out: bfloat16 [4096, 4096], P(('dp', 'expert'))
Inputs may be any that keep to these rules, and one draw needn't show every extreme that they name: `chosen`: token t lies in the rows of device t // 128 (devices numbered dp-major). Each expert's 128 indices are different; at most 8 of them lie in the rows of one device, and for every expert some device gives exactly 8.
All inputs are finite; a program needn't handle non-finite values.
Results may differ from a plain program's by a relative error of at most 0.0052.
Values may be sent and summed in bfloat16 or wider, within the bound.
A program may use at most 128 MiB of HBM per device.

v0:
```python
import jax
import jax.numpy as jnp
from jax import lax
from jax.sharding import PartitionSpec as P


def expert_rows(rows, w_gate, w_up, w_down):
    gated = jnp.dot(rows, w_gate, preferred_element_type=jnp.float32)
    lifted = jnp.dot(rows, w_up, preferred_element_type=jnp.float32)
    hidden = (jax.nn.silu(gated) * lifted).astype(jnp.bfloat16)
    return jnp.dot(hidden, w_down, preferred_element_type=jnp.float32).astype(jnp.bfloat16)


def slot_tables(levels, wanted, start_positions, slot_total, row_total):
    ranking = jnp.cumsum(wanted.astype(jnp.int32), axis=1) - 1
    slot_ids = jnp.arange(slot_total, dtype=jnp.int32)
    picks = wanted[:, :, None] & (ranking[:, :, None] == slot_ids[None, None, :])
    row_index = jnp.sum(jnp.where(picks, start_positions[:, :, None], 0), axis=1).reshape(-1)
    filled = jnp.any(picks, axis=1).reshape(-1)
    capacity_gating_weight = jnp.sum(jnp.where(picks, levels[:, :, None], 0.0), axis=1).reshape(-1)
    row_ids = jnp.arange(row_total, dtype=jnp.int32)
    member = (row_index[None, :] == row_ids[:, None]) & filled[None, :]
    selector = member.astype(jnp.bfloat16)
    weighted = jnp.where(member, capacity_gating_weight[None, :], 0.0).astype(jnp.bfloat16)
    return (selector, weighted)


def local(
    tokens,
    chosen,
    gate_levels,
    expert_gate,
    expert_up,
    expert_down,
    shared_gate,
    shared_up,
    shared_down,
):
    n_data = lax.axis_size("dp")
    n_expert = lax.axis_size("expert")
    accelerator_roster = n_data * n_expert
    tok_dev = tokens.shape[0]
    width = tokens.shape[1]
    slot_most = 2 * tok_dev // accelerator_roster
    row_data = lax.axis_index("dp")
    row_expert = lax.axis_index("expert")
    multiplier_factors = gate_levels.astype(jnp.float32) / 256.0
    pick_rows = (((0,), (0,)), ((), ()))
    contract = (((1,), (1,)), ((), ()))
    column = lax.all_gather(tokens, "dp", axis=0, tiled=True)
    gate_rows, up_rows, down_rows = (
        lax.all_gather(shared_gate, "expert", axis=0, tiled=True),
        lax.all_gather(shared_up, "expert", axis=0, tiled=True),
        lax.all_gather(shared_down, "expert", axis=0, tiled=True),
    )
    gated = lax.dot_general(column, gate_rows, contract, preferred_element_type=jnp.float32)
    lifted = lax.dot_general(column, up_rows, contract, preferred_element_type=jnp.float32)
    shared_hidden = (jax.nn.silu(gated) * lifted).astype(jnp.bfloat16)
    routed_own = None
    myself = row_data * n_expert + row_expert
    wanted = chosen // tok_dev == myself
    selector, weighted = slot_tables(
        multiplier_factors, wanted, chosen % tok_dev, slot_most, tok_dev
    )
    outgoing = lax.dot_general(selector, tokens, pick_rows, preferred_element_type=jnp.float32)
    outgoing, weighted = (outgoing.astype(jnp.bfloat16), weighted)
    outgoing = outgoing.reshape(accelerator_roster, slot_most, width)
    received = lax.all_to_all(outgoing, ("dp", "expert"), split_axis=0, concat_axis=0, tiled=True)
    flat = received.reshape(-1, width)
    returned = lax.all_to_all(
        expert_rows(flat, expert_gate[0], expert_up[0], expert_down[0]).reshape(received.shape),
        ("dp", "expert"),
        split_axis=0,
        concat_axis=0,
        tiled=True,
    )
    routed_own = jnp.dot(weighted, returned.reshape(-1, width), preferred_element_type=jnp.float32)
    value = jnp.dot(shared_hidden, down_rows, preferred_element_type=jnp.float32)
    combined = lax.psum_scatter(value, "dp", scatter_dimension=0, tiled=True)
    combined = combined + routed_own
    return combined.astype(jnp.bfloat16)


def solution(mesh):
    placed = (
        P(("dp", "expert"), None),
        P(),
        P(),
        P(("dp", "expert"), None, None),
        P(("dp", "expert"), None, None),
        P(("dp", "expert"), None, None),
        P(("dp", "expert"), None),
        P(("dp", "expert"), None),
        P(("dp", "expert"), None),
    )
    return jax.shard_map(
        local, mesh=mesh, in_specs=placed, out_specs=P(("dp", "expert"), None), check_vma=False
    )
```

profile of v0, /device:TPU:9, one launch (start us, length us, event | category | flops | bytes accessed | tf_op | source)
XLA Modules:
  0.0 521.2 jit_solution(7123957170573335426)
XLA Ops:
  6.5 0.0 all-gather.5.cloned.1.call-start
  6.5 0.7 all-gather.5.cloned.1.call-update
  7.3 0.0 all-gather.7.cloned.1.call-start
  7.3 0.7 all-gather.7.cloned.1.call-update
  8.0 0.0 all-gather.11.cloned.1.call-start
  8.1 0.7 all-gather.11.cloned.1.call-update
  8.7 0.0 all-gather.9.cloned.1.call-start
  8.8 0.5 all-gather.9.cloned.1.call-update
  9.3 0.0 reduce-scatter.2.cloned.1.call-start
  9.4 79.0 %all-gather.5.cloned.1.call-done = bf16[512,4096]{1,0:T(8,128)(2,1)} async-done(((bf16[128,4096]{1,0:T(8,128)(2,1)}), bf16[512,4096]{1,0:T(8,128)(2,1)}) %all-gather.5.cloned.1.call-update) | async-done | bytes 4194320 | tf_op jit(solution)/shard_map/all_gather | solution.py:50
  88.4 57.8 %all-gather.7.cloned.1.call-done = bf16[1024,4096]{1,0:T(8,128)(2,1)} async-done(((bf16[128,4096]{1,0:T(8,128)(2,1)}), bf16[1024,4096]{1,0:T(8,128)(2,1)}) %all-gather.7.cloned.1.call-update) | async-done | bytes 8388624 | tf_op jit(solution)/shard_map/all_gather | solution.py:52
  146.1 8.2 %fusion.49 = f32[512,1024]{1,0:T(8,128)S(1)} fusion(bf16[512,4096]{1,0:T(8,128)(2,1)} %all-gather.5.cloned.1.call-done, bf16[1024,4096]{1,0:T(8,128)(2,1)} %all-gather.7.cloned.1.call-done), kind=kOutput, calls=%fused_computation.47 | convolution fusion | flops 4294967296 | bytes 14680064 | tf_op jit(solution)/shard_map/dot_general | solution.py:56
  154.4 48.1 %all-gather.11.cloned.1.call-done = bf16[1024,4096]{1,0:T(8,128)(2,1)} async-done(((bf16[128,4096]{1,0:T(8,128)(2,1)}), bf16[1024,4096]{1,0:T(8,128)(2,1)}) %all-gather.11.cloned.1.call-update) | async-done | bytes 8388624 | tf_op jit(solution)/shard_map/all_gather | solution.py:54
  202.5 56.2 %all-gather.9.cloned.1.call-done = bf16[1024,4096]{1,0:T(8,128)(2,1)} async-done(((bf16[128,4096]{1,0:T(8,128)(2,1)}), bf16[1024,4096]{1,0:T(8,128)(2,1)}) %all-gather.9.cloned.1.call-update) | async-done | bytes 8388624 | tf_op jit(solution)/shard_map/all_gather | solution.py:53
  258.6 19.1 %fusion.50 = f32[512,4096]{1,0:T(8,128)} fusion(bf16[1024,4096]{1,0:T(8,128)(2,1)} %all-gather.11.cloned.1.call-done, f32[512,1024]{1,0:T(8,128)S(1)} %fusion.49, bf16[512,4096]{1,0:T(8,128)(2,1)} %all-gather.5.cloned.1.call-done, bf16[1024,4096]{1,0:T(8,128)(2,1)} %all-gather.9.cloned.1.call-done), kind=kOutput, calls=%fused_computation.48 | convolution fusion | flops 8593080320 | bytes 31457280 | tf_op jit(solution)/shard_map/dot_general | solution.py:78
  277.8 0.0 copy-start.1
  277.8 0.0 copy-start
  277.8 0.0 reduce-scatter.2.cloned.1.call-update
  277.8 0.7 copy-done.1
  278.5 0.3 reduce_window_sum.11
  278.8 0.6 select_reduce_fusion.1
  279.4 0.1 eq.41
  279.5 0.6 fusion.33
  280.1 0.1 and.34
  280.2 0.0 copy-done
  280.3 0.8 fusion.12
  281.0 106.4 %all_to_all.10 = bf16[32,8,4096]{2,1,0:T(8,128)(2,1)S(1)} all-to-all(bf16[32,8,4096]{2,1,0:T(8,128)(2,1)S(1)} %fusion.12), channel_id=1, replica_groups=mesh['dp'=4,'expert'=8] {'dp','expert'}, dimensions={0} | all-to-all | bytes 4194304 | tf_op jit(solution)/shard_map/all_to_all | solution.py:68
  387.4 4.6 fusion.4
  392.0 10.8 %fusion.9 = bf16[32,8,4096]{2,1,0:T(8,128)(2,1)} fusion(bf16[1,768,4096]{2,1,0:T(8,128)(2,1)} %param.14, bf16[1,4096,768]{2,1,0:T(8,128)(2,1)} %param.13, bf16[32,8,4096]{2,1,0:T(8,128)(2,1)S(1)} %all_to_all.10, f32[256,768]{1,0:T(8,128)S(1)} %fusion.4), kind=kOutput, calls=%fused_computation.8 | convolution fusion | flops 3223453696 | bytes 17563648 | tf_op jit(solution)/shard_map/dot_general | solution.py:11
  402.8 0.0 copy-start.2
  402.8 6.9 %all-to-all-start.1 = ((bf16[32,8,4096]{2,1,0:T(8,128)(2,1)}), bf16[32,8,4096]{2,1,0:T(8,128)(2,1)S(1)}, u32[]{:S(2)}, u32[]{:S(2)}) async-start(bf16[32,8,4096]{2,1,0:T(8,128)(2,1)} %fusion.9), calls=%async_computation.2 | async-start | bytes 4194304 | tf_op jit(solution)/shard_map/all_to_all | solution.py:70
  409.7 0.0 copy-done.2
  409.8 0.1 select_reduce_fusion
  409.9 0.1 broadcast_in_dim.48
  410.0 90.3 %all-to-all-done.1 = bf16[32,8,4096]{2,1,0:T(8,128)(2,1)S(1)} async-done(((bf16[32,8,4096]{2,1,0:T(8,128)(2,1)}), bf16[32,8,4096]{2,1,0:T(8,128)(2,1)S(1)}, u32[]{:S(2)}, u32[]{:S(2)}) %all-to-all-start.1) | async-done | bytes 2097184 | tf_op jit(solution)/shard_map/all_to_all | solution.py:70
  500.2 11.4 %reduce-scatter.2.cloned.1.call-done = f32[128,4096]{1,0:T(8,128)} async-done(((f32[512,4096]{1,0:T(8,128)}), f32[128,4096]{1,0:T(8,128)}) %reduce-scatter.2.cloned.1.call-update) | async-done | bytes 2097168 | tf_op jit(solution)/shard_map/reduce_scatter | solution.py:79
  511.6 3.1 fusion.13
  (3 shorter events, 0.0 us)
Async XLA Ops:
  6.5 81.8 %all-gather.5.cloned.1.call-start = ((), (), s32[]{:S(2)}) async-start(), calls=%async_computation.3 | async-start | bytes 5242880 | tf_op jit(solution)/shard_map/all_gather | solution.py:50
  7.3 138.9 %all-gather.7.cloned.1.call-start = ((), (), s32[]{:S(2)}) async-start(), calls=%async_computation.4 | async-start | bytes 9437184 | tf_op jit(solution)/shard_map/all_gather | solution.py:52
  8.0 194.5 %all-gather.11.cloned.1.call-start = ((), (), s32[]{:S(2)}) async-start(), calls=%async_computation.6 | async-start | bytes 9437184 | tf_op jit(solution)/shard_map/all_gather | solution.py:54
  8.7 249.9 %all-gather.9.cloned.1.call-start = ((), (), s32[]{:S(2)}) async-start(), calls=%async_computation.5 | async-start | bytes 9437184 | tf_op jit(solution)/shard_map/all_gather | solution.py:53
  9.3 502.3 %reduce-scatter.2.cloned.1.call-start = ((), (), s32[]{:S(2)}) async-start(), calls=%async_computation.7 | async-start | bytes 10485760 | tf_op jit(solution)/shard_map/reduce_scatter | solution.py:79
  277.8 0.7 copy-start.1
  277.8 2.5 copy-start
  402.8 7.0 %copy-start.2 = (s32[32,128]{1,0:T(8,128)S(1)}, s32[32,128]{1,0:T(8,128)}, u32[]{:S(2)}) copy-start(s32[32,128]{1,0:T(8,128)} %param.11) | copy-start | bytes 49156
  402.8 97.5 %all-to-all-start.1 = ((bf16[32,8,4096]{2,1,0:T(8,128)(2,1)}), bf16[32,8,4096]{2,1,0:T(8,128)(2,1)S(1)}, u32[]{:S(2)}, u32[]{:S(2)}) async-start(bf16[32,8,4096]{2,1,0:T(8,128)(2,1)} %fusion.9), calls=%async_computation.2 | async-start | bytes 4194304 | tf_op jit(solution)/shard_map/all_to_all | solution.py:70
Sparse Core Ops, SparseCore 0:
  8.9 79.3 all-gather.4
  90.2 55.8 all-gather.6
  148.0 54.3 all-gather.10
  204.2 54.3 all-gather.8
  277.9 233.6 reduce-scatter.1
where the time goes:
time: 522 us; the launch traced here: 521 us
  waiting for transfers between devices  345 us (66%)
  blocking collectives  106 us (20%)
  matrix products  46.6 us (9%)
  between operations  13.2 us (3%)
  starting transfers between devices  7.1 us (1%)
    all_to_all x1, blocking collectives, local(): lax.all_to_all(outgoing, ('dp', 'expert'), split_axis=0, concat_axis=0, t...  106 us
    all_to_all x1, waiting for transfers between devices, local(): lax.all_to_all(expert_rows(flat, expert_gate[0], expert_up[0], expert_dow...  90.3 us
    all_gather x1, waiting for transfers between devices, local(): column = lax.all_gather(tokens, 'dp', axis=0, tiled=True)  79 us
    all_gather x1, waiting for transfers between devices, local(): lax.all_gather(shared_gate, 'expert', axis=0, tiled=True)  57.8 us
    all_gather x1, waiting for transfers between devices, local(): lax.all_gather(shared_up, 'expert', axis=0, tiled=True)  56.2 us
    all_gather x1, waiting for transfers between devices, local(): lax.all_gather(shared_down, 'expert', axis=0, tiled=True)  48.1 us
    dot_general x1, matrix products, local(): jnp.dot(shared_hidden, down_rows, preferred_element_type=jnp.float32)  19.1 us
    reduce_scatter x1, waiting for transfers between devices, local(): combined = lax.psum_scatter(value, 'dp', scatter_dimension=0, tiled=True)  11.4 us
  transfers between devices with their start and end apart: 6, of which 6 were waited for; matrix products, arithmetic and copies ran while one was open for 5% of the time, Pallas kernels for 0%

commit v1 on v0

--- a/solution.py
+++ b/solution.py
@@ -47,7 +47,12 @@
     multiplier_factors = gate_levels.astype(jnp.float32) / 256.0
     pick_rows = (((0,), (0,)), ((), ()))
     contract = (((1,), (1,)), ((), ()))
-    column = lax.all_gather(tokens, "dp", axis=0, tiled=True)
+    ring = [tokens]
+    for hop in range(3):
+        ring.append(lax.ppermute(ring[-1], "dp", [(dev, (dev + 1) % 4) for dev in range(4)]))
+    column = jnp.roll(
+        jnp.concatenate(ring[::-1], axis=0), (lax.axis_index("dp") + 1) * ring[0].shape[0], axis=0
+    )
     gate_rows, up_rows, down_rows = (
         lax.all_gather(shared_gate, "expert", axis=0, tiled=True),
         lax.all_gather(shared_up, "expert", axis=0, tiled=True),

time: 522 us -> 441 us (0.84)
  waiting for transfers between devices: 345 us -> 250 us
  local copies, waits for them, and re-layouts: 0.99 us -> 12.1 us
    all_gather x1 -> x0, waiting for transfers between devices: 79 us -> none  [local(): column = lax.all_gather(tokens, 'dp', axis=0, tiled=True)]
    ppermute x0 -> x3, waiting for transfers between devices: none -> 70.7 us  [local(): lax.ppermute(ring[-1], 'dp', [(dev, (dev + 1) % 4) for dev in range(4)])]
    all_gather x1, waiting for transfers between devices: 56.2 us -> 0.01 us  [local(): lax.all_gather(shared_up, 'expert', axis=0, tiled=True)]
    all_gather x1, waiting for transfers between devices: 57.8 us -> 19 us  [local(): lax.all_gather(shared_gate, 'expert', axis=0, tiled=True)]
    unnamed x6 -> x13, local copies, waits for them, and re-layouts: 0.69 us -> 10.7 us
    all_gather x1, waiting for transfers between devices: 48.1 us -> 56.3 us  [local(): lax.all_gather(shared_down, 'expert', axis=0, tiled=True)]
  transfers between devices with their start and end apart: 6 -> 8, of which waited for: 6 -> 7; matrix products, arithmetic and copies ran while one was open for 5% -> 9% of each run, Pallas kernels for 0% -> 0%
where the time goes in v1:
time: 441 us
  waiting for transfers between devices  250 us (57%)
  blocking collectives  106 us (24%)
  matrix products  47.8 us (11%)
  between operations  13.2 us (3%)
  local copies, waits for them, and re-layouts  12.1 us (3%)
  starting transfers between devices  9.62 us (2%)
    all_to_all x1, blocking collectives, local(): lax.all_to_all(outgoing, ('dp', 'expert'), split_axis=0, concat_axis=0, t...  106 us
    all_to_all x1, waiting for transfers between devices, local(): lax.all_to_all(expert_rows(flat, expert_gate[0], expert_up[0], expert_dow...  90.3 us
    ppermute x3, waiting for transfers between devices, local(): lax.ppermute(ring[-1], 'dp', [(dev, (dev + 1) % 4) for dev in range(4)])  70.7 us
    all_gather x1, waiting for transfers between devices, local(): lax.all_gather(shared_down, 'expert', axis=0, tiled=True)  56.3 us
    dot_general x1, matrix products, local(): jnp.dot(shared_hidden, down_rows, preferred_element_type=jnp.float32)  19.3 us
    all_gather x1, waiting for transfers between devices, local(): lax.all_gather(shared_gate, 'expert', axis=0, tiled=True)  19 us
    reduce_scatter x1, waiting for transfers between devices, local(): combined = lax.psum_scatter(value, 'dp', scatter_dimension=0, tiled=True)  11.4 us
    dot_general x1, matrix products, expert_rows(): jnp.dot(hidden, w_down, preferred_element_type=jnp.float32)  10.8 us
  transfers between devices with their start and end apart: 8, of which 7 were waited for; matrix products, arithmetic and copies ran while one was open for 9% of the time, Pallas kernels for 0%

profile of v1, /device:TPU:9, one launch (start us, length us, event | category | flops | bytes accessed | tf_op | source)
XLA Modules:
  0.0 440.6 jit_solution(18011239342145070861)
XLA Ops:
  6.5 0.0 copy-start
  6.5 0.0 all-gather.6.cloned.1.call-start
  6.5 0.7 all-gather.6.cloned.1.call-update
  7.3 0.0 all-gather.4.cloned.1.call-start
  7.3 0.7 all-gather.4.cloned.1.call-update
  8.0 0.0 all-gather.8.cloned.1.call-start
  8.1 0.7 all-gather.8.cloned.1.call-update
  8.7 0.0 reduce-scatter.2.cloned.1.call-start
  8.8 1.3 collective-permute-start
  10.1 23.0 %collective-permute-done = bf16[128,4096]{1,0:T(8,128)(2,1)S(1)} collective-permute-done((bf16[128,4096]{1,0:T(8,128)(2,1)}, bf16[128,4096]{1,0:T(8,128)(2,1)S(1)}, u32[]{:S(2)}, u32[]{:S(2)}) %collective-permute-start) | collective-permute-done | bytes 1048608 | tf_op jit(solution)/shard_map/ppermute | solution.py:52
  33.2 1.2 collective-permute-start.1
  34.4 23.4 %collective-permute-done.1 = bf16[128,4096]{1,0:T(8,128)(2,1)S(1)} collective-permute-done((bf16[128,4096]{1,0:T(8,128)(2,1)S(1)}, bf16[128,4096]{1,0:T(8,128)(2,1)S(1)}, u32[]{:S(2)}, u32[]{:S(2)}) %collective-permute-start.1) | collective-permute-done | bytes 1048608 | tf_op jit(solution)/shard_map/ppermute | solution.py:52
  57.8 0.0 collective-permute-start.2
  57.8 24.3 %collective-permute-done.2 = bf16[128,4096]{1,0:T(8,128)(2,1)} collective-permute-done((bf16[128,4096]{1,0:T(8,128)(2,1)S(1)}, bf16[128,4096]{1,0:T(8,128)(2,1)}, u32[]{:S(2)}, u32[]{:S(2)}) %collective-permute-start.2) | collective-permute-done | bytes 1048608 | tf_op jit(solution)/shard_map/ppermute | solution.py:52
  82.1 2.4 constant_dynamic-update-slice_fusion.7
  84.4 1.0 constant_dynamic-update-slice_fusion.6
  85.5 1.0 constant_dynamic-update-slice_fusion.5
  86.5 0.0 copy-done
  86.5 1.1 constant_dynamic-update-slice_fusion.4
  87.6 2.4 constant_dynamic-update-slice_fusion.3
  90.0 1.0 constant_dynamic-update-slice_fusion.2
  91.0 1.1 constant_dynamic-update-slice_fusion.1
  92.1 1.1 constant_dynamic-update-slice_fusion
  93.2 0.0 all-gather.6.cloned.1.call-done
  93.2 9.4 %fusion.14 = f32[512,1024]{1,0:T(8,128)S(1)} fusion(bf16[1024,4096]{1,0:T(8,128)(2,1)} %all-gather.6.cloned.1.call-done, bf16[1024,4096]{1,0:T(8,128)(2,1)} %constant_dynamic-update-slice_fusion, s32[]{:T(128)S(6)} %select_n.37), kind=kOutput, calls=%fused_computation.12 | convolution fusion | flops 4294967296 | bytes 14680068 | tf_op jit(solution)/shard_map/dot_general | solution.py:62
  102.6 19.0 %all-gather.4.cloned.1.call-done = bf16[1024,4096]{1,0:T(8,128)(2,1)} async-done(((bf16[128,4096]{1,0:T(8,128)(2,1)}), bf16[1024,4096]{1,0:T(8,128)(2,1)}) %all-gather.4.cloned.1.call-update) | async-done | bytes 8388624 | tf_op jit(solution)/shard_map/all_gather | solution.py:57
  121.6 56.3 %all-gather.8.cloned.1.call-done = bf16[1024,4096]{1,0:T(8,128)(2,1)} async-done(((bf16[128,4096]{1,0:T(8,128)(2,1)}), bf16[1024,4096]{1,0:T(8,128)(2,1)}) %all-gather.8.cloned.1.call-update) | async-done | bytes 8388624 | tf_op jit(solution)/shard_map/all_gather | solution.py:59
  177.9 19.3 %fusion.31 = f32[512,4096]{1,0:T(8,128)} fusion(bf16[1024,4096]{1,0:T(8,128)(2,1)} %all-gather.8.cloned.1.call-done, f32[512,1024]{1,0:T(8,128)S(1)} %fusion.14, bf16[1024,4096]{1,0:T(8,128)(2,1)} %all-gather.4.cloned.1.call-done, bf16[1024,4096]{1,0:T(8,128)(2,1)} %constant_dynamic-update-slice_fusion, s32[]{:T(128)S(6)} %select_n.37), kind=kOutput, calls=%fused_computation.22 | convolution fusion | flops 8593080320 | bytes 31457284 | tf_op jit(solution)/shard_map/dot_general | solution.py:83
  197.1 0.0 copy-start.1
  197.2 0.0 reduce-scatter.2.cloned.1.call-update
  197.2 0.7 copy-done.1
  197.9 0.3 reduce_window_sum.11
  198.2 0.6 select_reduce_fusion.1
  198.8 0.1 eq.44
  198.9 0.6 fusion.43
  199.5 0.1 and.41
  199.6 0.8 fusion.12
  200.4 106.4 %all_to_all.10 = bf16[32,8,4096]{2,1,0:T(8,128)(2,1)S(1)} all-to-all(bf16[32,8,4096]{2,1,0:T(8,128)(2,1)S(1)} %fusion.12), channel_id=1, replica_groups=mesh['dp'=4,'expert'=8] {'dp','expert'}, dimensions={0} | all-to-all | bytes 4194304 | tf_op jit(solution)/shard_map/all_to_all | solution.py:73
  306.8 4.6 %fusion.4 = f32[256,768]{1,0:T(8,128)S(1)} fusion(bf16[1,4096,768]{2,1,0:T(8,128)(2,1)} %param.12, bf16[32,8,4096]{2,1,0:T(8,128)(2,1)S(1)} %all_to_all.10), kind=kOutput, calls=%fused_computation.4 | convolution fusion | flops 1610612736 | bytes 9175040 | tf_op jit(solution)/shard_map/dot_general | solution.py:8
  311.4 0.0 copy-start.2
  311.4 10.8 %fusion.9 = bf16[32,8,4096]{2,1,0:T(8,128)(2,1)} fusion(bf16[1,768,4096]{2,1,0:T(8,128)(2,1)} %param.14, bf16[1,4096,768]{2,1,0:T(8,128)(2,1)} %param.13, bf16[32,8,4096]{2,1,0:T(8,128)(2,1)S(1)} %all_to_all.10, f32[256,768]{1,0:T(8,128)S(1)} %fusion.4), kind=kOutput, calls=%fused_computation.8 | convolution fusion | flops 3223453696 | bytes 17563648 | tf_op jit(solution)/shard_map/dot_general | solution.py:11
  322.2 6.9 %all-to-all-start.1 = ((bf16[32,8,4096]{2,1,0:T(8,128)(2,1)}), bf16[32,8,4096]{2,1,0:T(8,128)(2,1)S(1)}, u32[]{:S(2)}, u32[]{:S(2)}) async-start(bf16[32,8,4096]{2,1,0:T(8,128)(2,1)} %fusion.9), calls=%async_computation.2 | async-start | bytes 4194304 | tf_op jit(solution)/shard_map/all_to_all | solution.py:75
  329.1 0.0 copy-done.2
  329.1 0.1 select_reduce_fusion
  329.3 0.1 broadcast_in_dim.48
  329.4 90.3 %all-to-all-done.1 = bf16[32,8,4096]{2,1,0:T(8,128)(2,1)S(1)} async-done(((bf16[32,8,4096]{2,1,0:T(8,128)(2,1)}), bf16[32,8,4096]{2,1,0:T(8,128)(2,1)S(1)}, u32[]{:S(2)}, u32[]{:S(2)}) %all-to-all-start.1) | async-done | bytes 2097184 | tf_op jit(solution)/shard_map/all_to_all | solution.py:75
  419.6 11.4 %reduce-scatter.2.cloned.1.call-done = f32[128,4096]{1,0:T(8,128)} async-done(((f32[512,4096]{1,0:T(8,128)}), f32[128,4096]{1,0:T(8,128)}) %reduce-scatter.2.cloned.1.call-update) | async-done | bytes 2097168 | tf_op jit(solution)/shard_map/reduce_scatter | solution.py:84
  431.0 3.1 fusion.13
  (4 shorter events, 0.0 us)
Async XLA Ops:
  6.5 80.0 %copy-start = (bf16[128,4096]{1,0:T(8,128)(2,1)S(1)}, bf16[128,4096]{1,0:T(8,128)(2,1)}, u32[]{:S(2)}) copy-start(bf16[128,4096]{1,0:T(8,128)(2,1)} %param.9) | copy-start | bytes 3145732
  6.5 86.7 %all-gather.6.cloned.1.call-start = ((), (), s32[]{:S(2)}) async-start(), calls=%async_computation.4 | async-start | bytes 9437184 | tf_op jit(solution)/shard_map/all_gather | solution.py:58
  7.3 114.3 %all-gather.4.cloned.1.call-start = ((), (), s32[]{:S(2)}) async-start(), calls=%async_computation.3 | async-start | bytes 9437184 | tf_op jit(solution)/shard_map/all_gather | solution.py:57
  8.0 169.9 %all-gather.8.cloned.1.call-start = ((), (), s32[]{:S(2)}) async-start(), calls=%async_computation.5 | async-start | bytes 9437184 | tf_op jit(solution)/shard_map/all_gather | solution.py:59
  8.7 422.3 %reduce-scatter.2.cloned.1.call-start = ((), (), s32[]{:S(2)}) async-start(), calls=%async_computation.6 | async-start | bytes 10485760 | tf_op jit(solution)/shard_map/reduce_scatter | solution.py:84
  8.8 24.4 %collective-permute-start = (bf16[128,4096]{1,0:T(8,128)(2,1)}, bf16[128,4096]{1,0:T(8,128)(2,1)S(1)}, u32[]{:S(2)}, u32[]{:S(2)}) collective-permute-start(bf16[128,4096]{1,0:T(8,128)(2,1)} %param.9), channel_id=1, source_target_pairs={{0,8},{8,16},{16,24},{24,0},{1,9},{9,17},{17,25},{25,1},{2,10},{10... | collective-permute-start | bytes 3145736 | tf_op jit(solution)/shard_map/ppermute | solution.py:52
  33.2 24.6 %collective-permute-start.1 = (bf16[128,4096]{1,0:T(8,128)(2,1)S(1)}, bf16[128,4096]{1,0:T(8,128)(2,1)S(1)}, u32[]{:S(2)}, u32[]{:S(2)}) collective-permute-start(bf16[128,4096]{1,0:T(8,128)(2,1)S(1)} %collective-permute-done), channel_id=1, source_target_pairs={{0,8},{8,16},{16,24},{24,0},{1,9},{9,17},{17,25},{25,1},{2,10},{10... | collective-permute-start | bytes 3145736 | tf_op jit(solution)/shard_map/ppermute | solution.py:52
  57.8 24.3 %collective-permute-start.2 = (bf16[128,4096]{1,0:T(8,128)(2,1)S(1)}, bf16[128,4096]{1,0:T(8,128)(2,1)}, u32[]{:S(2)}, u32[]{:S(2)}) collective-permute-start(bf16[128,4096]{1,0:T(8,128)(2,1)S(1)} %collective-permute-done.1), channel_id=1, source_target_pairs={{0,8},{8,16},{16,24},{24,0},{1,9},{9,17},{17,25},{25,1},{2,10},{10... | collective-permute-start | bytes 3145736 | tf_op jit(solution)/shard_map/ppermute | solution.py:52
  197.1 0.7 copy-start.1
  311.4 17.7 %copy-start.2 = (s32[32,128]{1,0:T(8,128)S(1)}, s32[32,128]{1,0:T(8,128)}, u32[]{:S(2)}) copy-start(s32[32,128]{1,0:T(8,128)} %param.11) | copy-start | bytes 49156
  322.2 97.5 %all-to-all-start.1 = ((bf16[32,8,4096]{2,1,0:T(8,128)(2,1)}), bf16[32,8,4096]{2,1,0:T(8,128)(2,1)S(1)}, u32[]{:S(2)}, u32[]{:S(2)}) async-start(bf16[32,8,4096]{2,1,0:T(8,128)(2,1)} %fusion.9), calls=%async_computation.2 | async-start | bytes 4194304 | tf_op jit(solution)/shard_map/all_to_all | solution.py:75
Sparse Core Ops, SparseCore 0:
  9.2 55.9 all-gather.5
  67.1 54.3 all-gather.3
  123.5 54.3 all-gather.7
  197.3 233.6 reduce-scatter.1
